TPU v7x, 128 devices: a whole 4x4x4 slice. The times are simulated.
128 devices in a mesh: pix: 64 (over x, z, y_hi, core), col: 2 (over y_lo).
Axes of the slice: x: 4, y: 4 (y_hi: 2, y_lo: 2; y = y_hi * 2 + y_lo), z: 4, core: 2. Of those that a mesh axis runs over, the one named last changes fastest.
Arguments:
- observed: float32 [16384, 4096], P('pix', 'col'), may hold values from -40 to 40
- valid_mask: int32 [16384, 512], P('pix', 'col'), may hold values 0 or 1
- pix_factor: float32 [16384, 256], P('pix'), may hold values from -6 to 6
- col_factor: float32 [4096, 256], P('col'), may hold values from -0.375 to 0.375
Outputs:
- pix_next: float32 [16384, 256], P('pix')
- col_next: float32 [4096, 256], P('col')
- cloud: float32 [16384, 4096], P('pix', 'col')
All inputs are finite; a program needn't handle non-finite values. No bound on the sum of `valid_mask` on one device may be relied on, other than what follows from the above.
Results may differ from a plain program's by a relative error of at most 0.0003.
Values sent between devices are 32-bit elements; how exact they have to be, the bound alone decides.
A program may use at most 64 MiB of HBM per device.

v0:
```python
import jax
import jax.numpy as jnp
from jax import lax
from jax.sharding import PartitionSpec as P

BANDS = 8
WIDTH = 256
ITERS = 2
PASSES = 2
highest = lax.Precision.HIGHEST
threshold_scale = 1.0
diffusion = 0.2


def passed_along(block, axis, distance):
    devices = range(lax.axis_size(axis))
    route = [(i - distance, i) for i in devices if i - distance in devices]
    return lax.ppermute(block, axis, route)


def soft_cut(values, level):
    return jnp.sign(values) * jnp.maximum(jnp.abs(values) - level, 0.0)


def flux_of(diff, level):
    return diff / (1.0 + (diff / level) ** 2)


def level_of(residual, weight, total):
    spread = lax.psum(jnp.sum(weight * residual * residual), ("pix", "col"))
    return threshold_scale * jnp.sqrt(spread / total + 1e-06)


def smooth_pass(grid, level, strip_index, pix_count):
    has_north = strip_index > 0
    has_south = strip_index < pix_count - 1
    top_row = grid[0]
    bottom_row = grid[-1]
    north_rim = passed_along(bottom_row, "pix", 1)
    south_rim = passed_along(top_row, "pix", -1)
    north_rim = jnp.where(has_north, north_rim, top_row)
    south_rim = jnp.where(has_south, south_rim, bottom_row)
    north = jnp.concatenate([north_rim[None], grid[:-1]], axis=0)
    south = jnp.concatenate([grid[1:], south_rim[None]], axis=0)
    west = jnp.concatenate([grid[:, :1], grid[:, :-1]], axis=1)
    east = jnp.concatenate([grid[:, 1:], grid[:, -1:]], axis=1)
    summed = flux_of(north - grid, level) + flux_of(south - grid, level)
    summed = summed + flux_of(west - grid, level) + flux_of(east - grid, level)
    return grid + diffusion * summed


def per_device(observed, valid_mask, pix_factor, col_factor):
    pix_count = lax.axis_size("pix")
    col_count = lax.axis_size("col")
    pixels, columns = observed.shape
    dates = valid_mask.shape[1]
    weight = jnp.broadcast_to(
        valid_mask.astype(jnp.float32)[:, :, None], (pixels, dates, BANDS)
    ).reshape(pixels, columns)
    total = float(pixels * columns * pix_count * col_count)
    pix_fac = pix_factor
    col_fac = col_factor
    low_rank = jnp.dot(pix_fac, col_fac.T, precision=highest)
    for iteration in range(ITERS):
        residual = observed - low_rank
        level = level_of(residual, weight, total)
        sparse = weight * soft_cut(residual, level)
        misfit = weight * (sparse - residual)
        pix_grad = lax.psum(jnp.dot(misfit, col_fac, precision=highest), "col")
        change = jnp.dot(pix_grad, col_fac.T, precision=highest)
        norm_local = jnp.sum(pix_grad * pix_grad)
        curve_local = jnp.sum(weight * change * change)
        top_sum = lax.psum(norm_local, "pix")
        bottom_sum = lax.psum(curve_local, ("pix", "col"))
        step_pix = top_sum / bottom_sum
        pix_fac = pix_fac - step_pix * pix_grad
        low_rank = low_rank - step_pix * change
        misfit = weight * (sparse - (observed - low_rank))
        local_grad = lax.dot_general(
            misfit,
            pix_fac,
            (((0,), (0,)), ((), ())),
            precision=highest,
            preferred_element_type=jnp.float32,
        )
        col_grad = lax.psum(local_grad, "pix")
        shifted = jnp.dot(pix_fac, col_grad.T, precision=highest)
        norm_local = jnp.sum(col_grad * col_grad)
        curve_local = jnp.sum(weight * shifted * shifted)
        top_sum = lax.psum(norm_local, "col")
        bottom_sum = lax.psum(curve_local, ("pix", "col"))
        step_col = top_sum / bottom_sum
        col_fac = col_fac - step_col * col_grad
        low_rank = low_rank - step_col * shifted
    residual = observed - low_rank
    level = level_of(residual, weight, total)
    layer = weight * soft_cut(residual, level)
    strip_index = lax.axis_index("pix")
    grid = layer.reshape(pixels // WIDTH, WIDTH, columns)
    for sweep_index in range(PASSES):
        grid = smooth_pass(grid, level, strip_index, pix_count)
    return (pix_fac, col_fac, grid.reshape(pixels, columns))


def solution(mesh):
    in_specs = (P("pix", "col"), P("pix", "col"), P("pix", None), P("col", None))
    out_specs = (P("pix", None), P("col", None), P("pix", "col"))
    return jax.shard_map(
        per_device, mesh=mesh, in_specs=in_specs, out_specs=out_specs, check_vma=False
    )
```

profile of v0, /device:TPU:32, one launch (start us, length us, event | category | flops | bytes accessed | tf_op | source)
XLA Modules:
  0.0 2382.3 jit_solution(10405248718728174888)
XLA Ops:
  11.8 7.0 fusion
  18.7 65.8 %psum.105 = f32[]{:T(128)} all-reduce(f32[]{:T(128)} %get-tuple-element.8), channel_id=1, replica_groups=mesh['pix'=64,'col'=2] {'pix','col'}, use_global_device_ids=true, to_apply=%region_1.0 | all-reduce | flops 1 | bytes 8 | tf_op jit(solution)/shard_map/psum | solution.py:30
  85.2 5.7 fusion.20
  91.0 28.1 %all-reduce.5.cloned.1.call-done = f32[256,256]{1,0:T(8,128)} async-done(((f32[256,256]{1,0:T(8,128)}), f32[256,256]{1,0:T(8,128)}) %all-reduce.5.cloned.1.call-update) | async-done | bytes 262160 | tf_op jit(solution)/shard_map/psum | solution.py:69
  120.7 156.7 %psum.107 = f32[]{:T(128)} all-reduce(f32[]{:T(128)} %multiply_reduce_fusion.3), channel_id=1, replica_groups=mesh['pix'=64,'col'=2] {'pix'}, use_global_device_ids=true, to_apply=%region_4.0 | all-reduce | flops 1 | bytes 8 | tf_op jit(solution)/shard_map/psum | solution.py:73
  277.5 5.6 fusion.1
  283.1 72.4 %psum.108 = f32[]{:T(128)} all-reduce(f32[]{:T(128)} %get-tuple-element.19), channel_id=1, replica_groups=mesh['pix'=64,'col'=2] {'pix','col'}, use_global_device_ids=true, to_apply=%region_6.0 | all-reduce | flops 1 | bytes 8 | tf_op jit(solution)/shard_map/psum | solution.py:74
  356.8 9.0 fusion.16
  365.9 638.4 %all-reduce.7.cloned.1.call-done = f32[2048,256]{1,0:T(8,128)} async-done(((f32[2048,256]{1,0:T(8,128)}), f32[2048,256]{1,0:T(8,128)}) %all-reduce.7.cloned.1.call-update) | async-done | bytes 2097168 | tf_op jit(solution)/shard_map/psum | solution.py:86
  1007.0 5.5 psum.110
  1012.5 5.5 fusion.2
  1018.0 68.9 %psum.111 = f32[]{:T(128)} all-reduce(f32[]{:T(128)} %get-tuple-element.21), channel_id=1, replica_groups=mesh['pix'=64,'col'=2] {'pix','col'}, use_global_device_ids=true, to_apply=%region_11.0 | all-reduce | flops 1 | bytes 8 | tf_op jit(solution)/shard_map/psum | solution.py:91
  1088.2 7.4 fusion.3
  1095.6 64.8 %psum.112 = f32[]{:T(128)} all-reduce(f32[]{:T(128)} %get-tuple-element.5), channel_id=1, replica_groups=mesh['pix'=64,'col'=2] {'pix','col'}, use_global_device_ids=true, to_apply=%region_13.0 | all-reduce | flops 1 | bytes 8 | tf_op jit(solution)/shard_map/psum | solution.py:30
  1168.7 27.3 %all-reduce.9.cloned.1.call-done = f32[256,256]{1,0:T(8,128)} async-done(((f32[256,256]{1,0:T(8,128)}), f32[256,256]{1,0:T(8,128)}) %all-reduce.9.cloned.1.call-update) | async-done | bytes 262160 | tf_op jit(solution)/shard_map/psum | solution.py:69
  1197.6 156.7 %psum.114 = f32[]{:T(128)} all-reduce(f32[]{:T(128)} %multiply_reduce_fusion.2), channel_id=1, replica_groups=mesh['pix'=64,'col'=2] {'pix'}, use_global_device_ids=true, to_apply=%region_16.0 | all-reduce | flops 1 | bytes 8 | tf_op jit(solution)/shard_map/psum | solution.py:73
  1354.3 5.6 fusion.4
  1359.9 72.4 %psum.115 = f32[]{:T(128)} all-reduce(f32[]{:T(128)} %get-tuple-element.23), channel_id=1, replica_groups=mesh['pix'=64,'col'=2] {'pix','col'}, use_global_device_ids=true, to_apply=%region_18.0 | all-reduce | flops 1 | bytes 8 | tf_op jit(solution)/shard_map/psum | solution.py:74
  1433.8 9.1 fusion.7
  1442.9 638.5 %all-reduce.11.cloned.1.call-done = f32[2048,256]{1,0:T(8,128)} async-done(((f32[2048,256]{1,0:T(8,128)}), f32[2048,256]{1,0:T(8,128)}) %all-reduce.11.cloned.1.call-update) | async-done | bytes 2097168 | tf_op jit(solution)/shard_map/psum | solution.py:86
  2084.1 5.5 psum.117
  2089.7 5.5 fusion.5
  2095.2 69.0 %psum.118 = f32[]{:T(128)} all-reduce(f32[]{:T(128)} %get-tuple-element.25), channel_id=1, replica_groups=mesh['pix'=64,'col'=2] {'pix','col'}, use_global_device_ids=true, to_apply=%region_23.0 | all-reduce | flops 1 | bytes 8 | tf_op jit(solution)/shard_map/psum | solution.py:91
  2165.4 6.5 fusion.6
  2171.9 64.7 %psum.119 = f32[]{:T(128)} all-reduce(f32[]{:T(128)} %get-tuple-element.3), channel_id=1, replica_groups=mesh['pix'=64,'col'=2] {'pix','col'}, use_global_device_ids=true, to_apply=%region_25.0 | all-reduce | flops 1 | bytes 8 | tf_op jit(solution)/shard_map/psum | solution.py:30
  2237.3 3.7 multiply_multiply_fusion.7
  2241.0 3.5 collective-permute-start.1
  2249.9 38.5 %collective-permute-done.1 = f32[256,2048]{1,0:T(8,128)S(1)} collective-permute-done((f32[256,2048]{1,0:T(8,128)}, f32[256,2048]{1,0:T(8,128)S(1)}, u32[]{:S(2)}, u32[]{:S(2)}) %collective-permute-start.1) | collective-permute-done | bytes 2097184 | tf_op jit(solution)/shard_map/ppermute | solution.py:18
  2288.5 4.2 collective-permute-done
  2292.7 4.4 multiply_add_fusion.1
  2304.3 39.8 %collective-permute-done.3 = f32[256,2048]{1,0:T(8,128)S(1)} collective-permute-done((f32[256,2048]{1,0:T(8,128)S(1)}, f32[256,2048]{1,0:T(8,128)S(1)}, u32[]{:S(2)}, u32[]{:S(2)}) %collective-permute-start.3) | collective-permute-done | bytes 2097184 | tf_op jit(solution)/shard_map/ppermute | solution.py:18
  2344.1 27.9 %collective-permute-done.2 = f32[256,2048]{1,0:T(8,128)S(1)} collective-permute-done((f32[256,2048]{1,0:T(8,128)S(1)}, f32[256,2048]{1,0:T(8,128)S(1)}, u32[]{:S(2)}, u32[]{:S(2)}) %collective-permute-start.2) | collective-permute-done | bytes 2097184 | tf_op jit(solution)/shard_map/ppermute | solution.py:18
  (47 shorter events, 36.9 us)
Async XLA Ops:
  7.2 111.9 %all-reduce.5.cloned.1.call-start = ((), (), s32[]{:S(2)}) async-start(), calls=%async_computation | async-start | bytes 524288 | tf_op jit(solution)/shard_map/psum | solution.py:69
  9.8 2.0 copy-start.8
  91.0 913.3 %all-reduce.7.cloned.1.call-start = ((), (), s32[]{:S(2)}) async-start(), calls=%async_computation.1 | async-start | bytes 4194304 | tf_op jit(solution)/shard_map/psum | solution.py:86
  277.5 79.3 %copy-start.6 = (f32[256,256]{1,0:T(8,128)S(1)}, f32[256,256]{1,0:T(8,128)}, u32[]{:S(2)}) copy-start(f32[256,256]{1,0:T(8,128)} %all-reduce.5.cloned.1.call-done) | copy-start | bytes 786436
  365.8 830.2 %all-reduce.9.cloned.1.call-start = ((), (), s32[]{:S(2)}) async-start(), calls=%async_computation.2 | async-start | bytes 524288 | tf_op jit(solution)/shard_map/psum | solution.py:69
  1161.1 4.0 copy-start.3
  1163.8 1.4 copy-start
  1168.7 912.7 %all-reduce.11.cloned.1.call-start = ((), (), s32[]{:S(2)}) async-start(), calls=%async_computation.3 | async-start | bytes 4194304 | tf_op jit(solution)/shard_map/psum | solution.py:86
  1354.3 79.4 %copy-start.5 = (f32[256,256]{1,0:T(8,128)S(1)}, f32[256,256]{1,0:T(8,128)}, u32[]{:S(2)}) copy-start(f32[256,256]{1,0:T(8,128)} %all-reduce.9.cloned.1.call-done) | copy-start | bytes 786436
  1433.8 655.9 %copy-start.4 = (f32[256,256]{1,0:T(8,128)}, f32[256,256]{1,0:T(8,128)S(1)}, u32[]{:S(2)}) copy-start(f32[256,256]{1,0:T(8,128)S(1)} %multiply_subtract_fusion.7) | copy-start | bytes 786436
  2241.0 47.5 %collective-permute-start.1 = (f32[256,2048]{1,0:T(8,128)}, f32[256,2048]{1,0:T(8,128)S(1)}, u32[]{:S(2)}, u32[]{:S(2)}) collective-permute-start(f32[256,2048]{1,0:T(8,128)} %multiply_multiply_fusion.7), channel_id=1, source_target_pairs={{2,0},{4,2},{6,4},{8,6},{10,8},{12,10},{14,12},{16,14},{18,16},{20... | collective-permute-start | bytes 6291464 | tf_op jit(solution)/shard_map/ppermute | solution.py:18
  2244.6 48.2 %collective-permute-start = (f32[256,2048]{1,0:T(8,128)}, f32[256,2048]{1,0:T(8,128)}, u32[]{:S(2)}, u32[]{:S(2)}) collective-permute-start(f32[256,2048]{1,0:T(8,128)} %multiply_multiply_fusion.7), channel_id=1, source_target_pairs={{0,2},{2,4},{4,6},{6,8},{8,10},{10,12},{12,14},{14,16},{16,18},{18... | collective-permute-start | bytes 6291464 | tf_op jit(solution)/shard_map/ppermute | solution.py:18
  2288.5 4.3 copy-start.7
  2292.7 9.5 copy-start.1
  2292.7 9.5 copy-start.2
  2297.1 47.0 %collective-permute-start.3 = (f32[256,2048]{1,0:T(8,128)S(1)}, f32[256,2048]{1,0:T(8,128)S(1)}, u32[]{:S(2)}, u32[]{:S(2)}) collective-permute-start(f32[256,2048]{1,0:T(8,128)S(1)} %multiply_add_fusion.1), channel_id=1, source_target_pairs={{2,0},{4,2},{6,4},{8,6},{10,8},{12,10},{14,12},{16,14},{18,16},{20... | collective-permute-start | bytes 6291464 | tf_op jit(solution)/shard_map/ppermute | solution.py:18
  2300.3 71.6 %collective-permute-start.2 = (f32[256,2048]{1,0:T(8,128)S(1)}, f32[256,2048]{1,0:T(8,128)S(1)}, u32[]{:S(2)}, u32[]{:S(2)}) collective-permute-start(f32[256,2048]{1,0:T(8,128)S(1)} %multiply_add_fusion.1), channel_id=1, source_target_pairs={{0,2},{2,4},{4,6},{6,8},{8,10},{10,12},{12,14},{14,16},{16,18},{18... | collective-permute-start | bytes 6291464 | tf_op jit(solution)/shard_map/ppermute | solution.py:18
Sparse Core Ops, SparseCore 0:
  91.1 27.9 all-reduce.4
  366.0 638.2 all-reduce.6
  1168.8 27.1 all-reduce.8
  1443.0 638.2 all-reduce.10
where the time goes:
time: 2390 us; the launch traced here: 2380 us
  waiting for transfers between devices  1440 us (60%)
  blocking collectives  803 us (34%)
  matrix products  56.5 us (2%)
  other arithmetic  39.3 us (2%)
    psum x2, waiting for transfers between devices, per_device(): col_grad = lax.psum(local_grad, 'pix')  1280 us
    psum x2, blocking collectives, per_device(): top_sum = lax.psum(norm_local, 'pix')  313 us
    psum x4, blocking collectives, per_device(): bottom_sum = lax.psum(curve_local, ('pix', 'col'))  283 us
    psum x3, blocking collectives, level_of(): spread = lax.psum(jnp.sum(weight * residual * residual), ('pix', 'col'))  195 us
    ppermute x4, waiting for transfers between devices, passed_along(): return lax.ppermute(block, axis, route)  110 us
    psum x2, waiting for transfers between devices, per_device(): pix_grad = lax.psum(jnp.dot(misfit, col_fac, precision=highest), 'col')  55.3 us
  transfers between devices with their start and end apart: 8, of which 8 were waited for; matrix products, arithmetic and copies ran while one was open for 0% of the time, Pallas kernels for 0%

commit v1 on v0

--- a/solution.py
+++ b/solution.py
@@ -71,7 +71,7 @@
         norm_local = jnp.sum(pix_grad * pix_grad)
         curve_local = jnp.sum(weight * change * change)
         top_sum = lax.psum(norm_local, "pix")
-        bottom_sum = lax.psum(curve_local, ("pix", "col"))
+        bottom_sum = lax.psum(lax.psum(curve_local, "pix"), "col")
         step_pix = top_sum / bottom_sum
         pix_fac = pix_fac - step_pix * pix_grad
         low_rank = low_rank - step_pix * change

time: 2390 us -> 2270 us (0.950)
  blocking collectives: 803 us -> 669 us
    psum x4 -> x2, blocking collectives: 283 us -> 138 us  [per_device(): bottom_sum = lax.psum(curve_local, ('pix', 'col'))]
where the time goes in v1:
time: 2270 us; the launch traced here: 2260 us
  waiting for transfers between devices  1460 us (64%)
  blocking collectives  669 us (29%)
  matrix products  56.5 us (2%)
  other arithmetic  39.3 us (2%)
    psum x2, waiting for transfers between devices, per_device(): col_grad = lax.psum(local_grad, 'pix')  1290 us
    psum x2, blocking collectives, per_device(): top_sum = lax.psum(norm_local, 'pix')  314 us
    psum x3, blocking collectives, level_of(): spread = lax.psum(jnp.sum(weight * residual * residual), ('pix', 'col'))  195 us
    psum x2, blocking collectives, per_device(): bottom_sum = lax.psum(curve_local, ('pix', 'col'))  138 us
    ppermute x4, waiting for transfers between devices, passed_along(): return lax.ppermute(block, axis, route)  110 us
    psum x2, waiting for transfers between devices, per_device(): pix_grad = lax.psum(jnp.dot(misfit, col_fac, precision=highest), 'col')  55.3 us
  transfers between devices with their start and end apart: 8, of which 8 were waited for; matrix products, arithmetic and copies ran while one was open for 0% of the time, Pallas kernels for 0%

profile of v1, /device:TPU:32, one launch (start us, length us, event | category | flops | bytes accessed | tf_op | source)
XLA Modules:
  0.0 2262.6 jit_solution(14642473538224171193)
XLA Ops:
  11.8 7.0 fusion
  18.7 65.8 %psum.119 = f32[]{:T(128)} all-reduce(f32[]{:T(128)} %get-tuple-element.12), channel_id=1, replica_groups=mesh['pix'=64,'col'=2] {'pix','col'}, use_global_device_ids=true, to_apply=%region_1.0 | all-reduce | flops 1 | bytes 8 | tf_op jit(solution)/shard_map/psum | solution.py:30
  85.2 5.7 fusion.20
  91.0 28.1 %all-reduce.7.cloned.1.call-done = f32[256,256]{1,0:T(8,128)} async-done(((f32[256,256]{1,0:T(8,128)}), f32[256,256]{1,0:T(8,128)}) %all-reduce.7.cloned.1.call-update) | async-done | bytes 262160 | tf_op jit(solution)/shard_map/psum | solution.py:69
  120.7 5.6 fusion.1
  126.4 156.7 %all-reduce.1 = (f32[]{:T(128)}, f32[]{:T(128)}) all-reduce(f32[]{:T(128)} %multiply_reduce_fusion.3, f32[]{:T(128)} %get-tuple-element.23), channel_id=1, replica_groups=mesh['pix'=64,'col'=2] {'pix'}, use_global_device_ids=true, to_apply=%region_4.0 | all-reduce | flops 2 | bytes 16 | tf_op jit(solution)/shard_map/psum | solution.py:73
  283.1 6.0 psum.123
  290.4 9.0 fusion.16
  299.5 645.4 %all-reduce.9.cloned.1.call-done = f32[2048,256]{1,0:T(8,128)} async-done(((f32[2048,256]{1,0:T(8,128)}), f32[2048,256]{1,0:T(8,128)}) %all-reduce.9.cloned.1.call-update) | async-done | bytes 2097168 | tf_op jit(solution)/shard_map/psum | solution.py:86
  947.6 5.5 psum.125
  953.1 5.5 fusion.2
  958.6 68.9 %psum.126 = f32[]{:T(128)} all-reduce(f32[]{:T(128)} %get-tuple-element.25), channel_id=1, replica_groups=mesh['pix'=64,'col'=2] {'pix','col'}, use_global_device_ids=true, to_apply=%region_12.0 | all-reduce | flops 1 | bytes 8 | tf_op jit(solution)/shard_map/psum | solution.py:91
  1028.8 7.4 fusion.3
  1036.3 64.7 %psum.127 = f32[]{:T(128)} all-reduce(f32[]{:T(128)} %get-tuple-element.9), channel_id=1, replica_groups=mesh['pix'=64,'col'=2] {'pix','col'}, use_global_device_ids=true, to_apply=%region_14.0 | all-reduce | flops 1 | bytes 8 | tf_op jit(solution)/shard_map/psum | solution.py:30
  1109.3 27.3 %all-reduce.11.cloned.1.call-done = f32[256,256]{1,0:T(8,128)} async-done(((f32[256,256]{1,0:T(8,128)}), f32[256,256]{1,0:T(8,128)}) %all-reduce.11.cloned.1.call-update) | async-done | bytes 262160 | tf_op jit(solution)/shard_map/psum | solution.py:69
  1138.2 5.6 fusion.4
  1143.8 156.8 %all-reduce = (f32[]{:T(128)}, f32[]{:T(128)}) all-reduce(f32[]{:T(128)} %multiply_reduce_fusion.2, f32[]{:T(128)} %get-tuple-element.27), channel_id=1, replica_groups=mesh['pix'=64,'col'=2] {'pix'}, use_global_device_ids=true, to_apply=%region_17.0 | all-reduce | flops 2 | bytes 16 | tf_op jit(solution)/shard_map/psum | solution.py:73
  1300.6 5.5 psum.131
  1307.5 9.1 fusion.7
  1316.6 645.5 %all-reduce.13.cloned.1.call-done = f32[2048,256]{1,0:T(8,128)} async-done(((f32[2048,256]{1,0:T(8,128)}), f32[2048,256]{1,0:T(8,128)}) %all-reduce.13.cloned.1.call-update) | async-done | bytes 2097168 | tf_op jit(solution)/shard_map/psum | solution.py:86
  1964.8 5.8 psum.133
  1970.6 5.5 fusion.5
  1976.1 69.0 %psum.134 = f32[]{:T(128)} all-reduce(f32[]{:T(128)} %get-tuple-element.29), channel_id=1, replica_groups=mesh['pix'=64,'col'=2] {'pix','col'}, use_global_device_ids=true, to_apply=%region_25.0 | all-reduce | flops 1 | bytes 8 | tf_op jit(solution)/shard_map/psum | solution.py:91
  2046.3 6.5 fusion.6
  2052.8 64.4 %psum.135 = f32[]{:T(128)} all-reduce(f32[]{:T(128)} %get-tuple-element.7), channel_id=1, replica_groups=mesh['pix'=64,'col'=2] {'pix','col'}, use_global_device_ids=true, to_apply=%region_27.0 | all-reduce | flops 1 | bytes 8 | tf_op jit(solution)/shard_map/psum | solution.py:30
  2117.9 3.7 multiply_multiply_fusion.7
  2121.6 3.5 collective-permute-start.1
  2130.5 38.5 %collective-permute-done.1 = f32[256,2048]{1,0:T(8,128)S(1)} collective-permute-done((f32[256,2048]{1,0:T(8,128)}, f32[256,2048]{1,0:T(8,128)S(1)}, u32[]{:S(2)}, u32[]{:S(2)}) %collective-permute-start.1) | collective-permute-done | bytes 2097184 | tf_op jit(solution)/shard_map/ppermute | solution.py:18
  2169.1 4.2 collective-permute-done
  2173.3 4.4 multiply_add_fusion.1
  2184.9 39.8 %collective-permute-done.3 = f32[256,2048]{1,0:T(8,128)S(1)} collective-permute-done((f32[256,2048]{1,0:T(8,128)S(1)}, f32[256,2048]{1,0:T(8,128)S(1)}, u32[]{:S(2)}, u32[]{:S(2)}) %collective-permute-start.3) | collective-permute-done | bytes 2097184 | tf_op jit(solution)/shard_map/ppermute | solution.py:18
  2224.7 27.9 %collective-permute-done.2 = f32[256,2048]{1,0:T(8,128)S(1)} collective-permute-done((f32[256,2048]{1,0:T(8,128)S(1)}, f32[256,2048]{1,0:T(8,128)S(1)}, u32[]{:S(2)}, u32[]{:S(2)}) %collective-permute-start.2) | collective-permute-done | bytes 2097184 | tf_op jit(solution)/shard_map/ppermute | solution.py:18
  (47 shorter events, 36.9 us)
Async XLA Ops:
  7.2 111.9 %all-reduce.7.cloned.1.call-start = ((), (), s32[]{:S(2)}) async-start(), calls=%async_computation | async-start | bytes 524288 | tf_op jit(solution)/shard_map/psum | solution.py:69
  9.8 2.0 copy-start.8
  91.0 853.9 %all-reduce.9.cloned.1.call-start = ((), (), s32[]{:S(2)}) async-start(), calls=%async_computation.1 | async-start | bytes 4194304 | tf_op jit(solution)/shard_map/psum | solution.py:86
  120.7 169.6 %copy-start.6 = (f32[256,256]{1,0:T(8,128)S(1)}, f32[256,256]{1,0:T(8,128)}, u32[]{:S(2)}) copy-start(f32[256,256]{1,0:T(8,128)} %all-reduce.7.cloned.1.call-done) | copy-start | bytes 786436
  299.4 837.2 %all-reduce.11.cloned.1.call-start = ((), (), s32[]{:S(2)}) async-start(), calls=%async_computation.2 | async-start | bytes 524288 | tf_op jit(solution)/shard_map/psum | solution.py:69
  1101.7 4.0 copy-start.3
  1104.4 1.4 copy-start
  1109.3 852.8 %all-reduce.13.cloned.1.call-start = ((), (), s32[]{:S(2)}) async-start(), calls=%async_computation.3 | async-start | bytes 4194304 | tf_op jit(solution)/shard_map/psum | solution.py:86
  1138.2 169.2 %copy-start.5 = (f32[256,256]{1,0:T(8,128)S(1)}, f32[256,256]{1,0:T(8,128)}, u32[]{:S(2)}) copy-start(f32[256,256]{1,0:T(8,128)} %all-reduce.11.cloned.1.call-done) | copy-start | bytes 786436
  1307.5 663.1 %copy-start.4 = (f32[256,256]{1,0:T(8,128)}, f32[256,256]{1,0:T(8,128)S(1)}, u32[]{:S(2)}) copy-start(f32[256,256]{1,0:T(8,128)S(1)} %multiply_subtract_fusion.7) | copy-start | bytes 786436
  2121.6 47.5 %collective-permute-start.1 = (f32[256,2048]{1,0:T(8,128)}, f32[256,2048]{1,0:T(8,128)S(1)}, u32[]{:S(2)}, u32[]{:S(2)}) collective-permute-start(f32[256,2048]{1,0:T(8,128)} %multiply_multiply_fusion.7), channel_id=1, source_target_pairs={{2,0},{4,2},{6,4},{8,6},{10,8},{12,10},{14,12},{16,14},{18,16},{20... | collective-permute-start | bytes 6291464 | tf_op jit(solution)/shard_map/ppermute | solution.py:18
  2125.2 48.2 %collective-permute-start = (f32[256,2048]{1,0:T(8,128)}, f32[256,2048]{1,0:T(8,128)}, u32[]{:S(2)}, u32[]{:S(2)}) collective-permute-start(f32[256,2048]{1,0:T(8,128)} %multiply_multiply_fusion.7), channel_id=1, source_target_pairs={{0,2},{2,4},{4,6},{6,8},{8,10},{10,12},{12,14},{14,16},{16,18},{18... | collective-permute-start | bytes 6291464 | tf_op jit(solution)/shard_map/ppermute | solution.py:18
  2169.1 4.3 copy-start.7
  2173.3 9.5 copy-start.1
  2173.3 9.5 copy-start.2
  2177.7 47.0 %collective-permute-start.3 = (f32[256,2048]{1,0:T(8,128)S(1)}, f32[256,2048]{1,0:T(8,128)S(1)}, u32[]{:S(2)}, u32[]{:S(2)}) collective-permute-start(f32[256,2048]{1,0:T(8,128)S(1)} %multiply_add_fusion.1), channel_id=1, source_target_pairs={{2,0},{4,2},{6,4},{8,6},{10,8},{12,10},{14,12},{16,14},{18,16},{20... | collective-permute-start | bytes 6291464 | tf_op jit(solution)/shard_map/ppermute | solution.py:18
  2180.9 71.6 %collective-permute-start.2 = (f32[256,2048]{1,0:T(8,128)S(1)}, f32[256,2048]{1,0:T(8,128)S(1)}, u32[]{:S(2)}, u32[]{:S(2)}) collective-permute-start(f32[256,2048]{1,0:T(8,128)S(1)} %multiply_add_fusion.1), channel_id=1, source_target_pairs={{0,2},{2,4},{4,6},{6,8},{8,10},{10,12},{12,14},{14,16},{16,18},{18... | collective-permute-start | bytes 6291464 | tf_op jit(solution)/shard_map/ppermute | solution.py:18
Sparse Core Ops, SparseCore 0:
  91.1 27.9 all-reduce.6
  299.5 645.2 all-reduce.8
  1109.4 27.1 all-reduce.10
  1316.7 645.2 all-reduce.12
